TPU v7x, 32 devices: a whole 2x2x4 slice. The times are simulated.
32 devices in a mesh: comp: 4 (over y, core), gx: 2 (over x), gy: 4 (over z).
Axes of the slice: x: 2, y: 2, z: 4, core: 2. Of those that a mesh axis runs over, the one named last changes fastest.
Arguments:
- field: float32 [4, 256, 64, 256], P('comp', 'gx', 'gy'), may hold values from -6 to 6
- third_level: int32 [4], replicated, may hold values from 2 to 6
- coefficients: int32 [4], replicated, may hold values from -3 to 3, as said below
- rates: float32 [2, 4], replicated, may hold values from 0.01 to 0.4, as said below
- reaction: float32 [1], replicated, may hold values from 0.1 to 0.3
Outputs:
- result: float32 [4, 256, 64, 256], P('comp', 'gx', 'gy')
Inputs may be any that keep to these rules, and one draw needn't show every extreme that they name: The fourth dimension of grid g has level 8 minus third_level[g]. `coefficients`: every weight is a nonzero integer; some are positive and some negative. `rates`: courant numbers of the first two dimensions lie from 0.3 to 0.4, all other entries from 0.01 to 0.02.
All inputs are finite; a program needn't handle non-finite values.
Results may differ from a plain program's by a relative error of at most 0.0003.
Values sent between devices are 32-bit elements; how exact they have to be, the bound alone decides.
No kernel may reach another device: no remote copies, remote signals or barrier semaphores. Data moves between devices by JAX's collectives and lax.ppermute only.
A program may use at most 128 MiB of HBM per device.

v0:
```python
import jax
import jax.numpy as jnp
import numpy as np
from jax import lax
from jax.sharding import PartitionSpec as P

SECTIONS = 4
LEVEL_SUM = 8


def extended(block, sides, width):
    for axis, dim in sides:
        count = lax.axis_size(axis)
        forward = [(i, i + 1) for i in range(count - 1)]
        forward.append((count - 1, 0))
        backward = [(target, source) for source, target in forward]
        low = lax.ppermute(
            lax.slice_in_dim(block, block.shape[dim] - width, None, axis=dim), axis, forward
        )
        high = lax.ppermute(lax.slice_in_dim(block, 0, width, axis=dim), axis, backward)
        block = jnp.concatenate([low, block, high], axis=dim)
    return block


def points(level):
    return 1 if level == 0 else 2 ** (level - 1)


def slot_table():
    top = LEVEL_SUM - 2
    table = np.zeros((top + 1) * (top + 1), np.int32)
    total = 0
    for first in range(top + 1):
        for second in range(top + 1):
            if first + second <= LEVEL_SUM:
                table[first * (top + 1) + second] = total
                total += points(first) * points(second)
    return (table, total)


def hier_level(index, level):
    zeros = jnp.zeros_like(index)
    for power in range(1, LEVEL_SUM + 1):
        zeros = zeros + (jnp.remainder(index, 2**power) == 0).astype(jnp.int32)
    depth = jnp.where(index == 0, 0, level - zeros)
    placed = jnp.where(index == 0, 0, jnp.right_shift(index, zeros + 1))
    return (depth, placed)


def fast_layout(level_a, size):
    level_b = LEVEL_SUM - level_a
    width = jnp.left_shift(jnp.int32(1), level_b)
    index = jnp.arange(size, dtype=jnp.int32)
    third = index // width
    return (width, third, index - third * width)


def slot_positions(level_a, table):
    top = LEVEL_SUM - 2
    size = 2**LEVEL_SUM
    width, third, fourth = fast_layout(level_a, size)
    depth_third, rank_third = hier_level(third, level_a)
    depth_fourth, rank_fourth = hier_level(fourth, LEVEL_SUM - level_a)
    count_fourth = jnp.where(
        depth_fourth == 0, 1, jnp.left_shift(jnp.int32(1), jnp.maximum(depth_fourth - 1, 0))
    )
    code = depth_third * (top + 1) + depth_fourth
    choose = code[:, None] == jnp.arange((top + 1) * (top + 1), dtype=jnp.int32)[None, :]
    offset = jnp.sum(jnp.where(choose, jnp.asarray(table)[None, :], 0), axis=1).astype(jnp.int32)
    return offset + rank_third * count_fourth + rank_fourth


def block_neighbours(values, shift, width, inner):
    ahead = jnp.where(
        inner + shift < width,
        jnp.roll(values, -shift, axis=-1),
        jnp.roll(values, width - shift, axis=-1),
    )
    behind = jnp.where(
        inner - shift >= 0,
        jnp.roll(values, shift, axis=-1),
        jnp.roll(values, shift - width, axis=-1),
    )
    return (ahead, behind)


def transform(values, level_a, forward):
    top = LEVEL_SUM - 2
    level_b = LEVEL_SUM - level_a
    width, third, fourth = fast_layout(level_a, values.shape[-1])
    depth_third = hier_level(third, level_a)[0]
    depth_fourth = hier_level(fourth, level_b)[0]
    factor = -0.5 if forward else 0.5

    def fourth_pass(values, level):
        shift = jnp.left_shift(jnp.int32(1), jnp.maximum(level_b - level, 0))
        ahead, behind = block_neighbours(values, shift, width, fourth)
        return jnp.where(depth_fourth == level, values + factor * (ahead + behind), values)

    def third_pass(values, level):
        shift = jnp.left_shift(jnp.int32(1), jnp.maximum(level_a - level, 0))
        ahead = jnp.roll(values, -shift * width, axis=-1)
        behind = jnp.roll(values, shift * width, axis=-1)
        return jnp.where(depth_third == level, values + factor * (ahead + behind), values)

    if forward:
        for level in range(top, 0, -1):
            values = fourth_pass(values, level)
        for level in range(top, 0, -1):
            values = third_pass(values, level)
    else:
        for level in range(1, top + 1):
            values = third_pass(values, level)
        for level in range(1, top + 1):
            values = fourth_pass(values, level)
    return values


def grid_rates(rates, level_a):
    top = LEVEL_SUM - 2
    level_b = LEVEL_SUM - level_a
    coarse_third = 1.0 / jnp.left_shift(jnp.int32(1), top - level_a).astype(jnp.float32)
    coarse_fourth = 1.0 / jnp.left_shift(jnp.int32(1), top - level_b).astype(jnp.float32)
    unity = jnp.ones((), jnp.float32)
    diffusion = rates[0] * jnp.stack(
        [unity, unity, coarse_third * coarse_third, coarse_fourth * coarse_fourth]
    )
    courant = rates[1] * jnp.stack([unity, unity, coarse_third, coarse_fourth])
    return (diffusion, courant)


def advance(padded, diffusion, courant, rate, width, fourth):
    centre = padded[1:-1, 1:-1]
    up_first = padded[2:, 1:-1]
    down_first = padded[:-2, 1:-1]
    up_second = padded[1:-1, 2:]
    down_second = padded[1:-1, :-2]
    up_third = jnp.roll(centre, -width, axis=-1)
    down_third = jnp.roll(centre, width, axis=-1)
    up_fourth, down_fourth = block_neighbours(centre, 1, width, fourth)
    change = diffusion[0] * (up_first - 2.0 * centre + down_first) - courant[0] * (
        centre - down_first
    )
    change = (
        change
        + diffusion[1] * (up_second - 2.0 * centre + down_second)
        - courant[1] * (centre - down_second)
    )
    change = (
        change
        + diffusion[2] * (up_third - 2.0 * centre + down_third)
        - courant[2] * (centre - down_third)
    )
    change = (
        change
        + diffusion[3] * (up_fourth - 2.0 * centre + down_fourth)
        - courant[3] * (centre - down_fourth)
    )
    return centre + change + rate * centre / (1.0 + centre * centre)


def local(field, third_level, coefficients, rates, reaction):
    grid = lax.axis_index("comp")
    level_a = lax.dynamic_index_in_dim(third_level, grid, 0, False)
    weight = lax.dynamic_index_in_dim(coefficients, grid, 0, False).astype(jnp.float32)
    diffusion, courant = grid_rates(rates, level_a)
    size = field.shape[-1]
    width, third, fourth = fast_layout(level_a, size)
    values = field[0]
    for section in range(SECTIONS):
        padded = extended(values, (("gx", 0), ("gy", 1)), 1)
        values = advance(padded, diffusion, courant, reaction[0], width, fourth)
    surplus = transform(values, level_a, True) * weight
    table, total_slots = slot_table()
    own_slots = slot_positions(level_a, table)
    columns = jnp.arange(size, dtype=jnp.int32)
    carry = jnp.zeros_like(surplus)
    piece = lax.all_gather(surplus[None], "comp", axis=0, tiled=True)

    def add_grid(inner, item):
        remote, source_grid = item
        other_level = lax.dynamic_index_in_dim(third_level, source_grid, 0, False)
        other_slots = slot_positions(other_level, table)
        match = other_slots[None, :] == own_slots[:, None]
        source = jnp.sum(jnp.where(match, columns[None, :], 0), axis=1)
        found = jnp.any(match, axis=1)
        return (inner + jnp.where(found, jnp.take(remote, source, axis=-1), 0.0), None)

    sources = jnp.arange(piece.shape[0], dtype=jnp.int32)
    carry, unused = lax.scan(add_grid, carry, (piece, sources))
    return transform(carry, level_a, False)[None]


def solution(mesh):
    return jax.shard_map(
        local,
        mesh=mesh,
        in_specs=(P("comp", "gx", "gy", None), P(), P(), P(), P()),
        out_specs=P("comp", "gx", "gy", None),
        check_vma=False,
    )
```

profile of v0, /device:TPU:0, one launch (start us, length us, event | category | flops | bytes accessed | tf_op | source)
XLA Modules:
  0.0 363.2 jit_solution(3005916287803881157)
XLA Ops:
  7.3 3.0 collective-permute-start.1
  15.1 3.0 fusion.314
  18.1 2.8 fusion.315
  31.7 4.1 %collective-permute-start.2 = (f32[130,1,256]{2,1,0:T(1,128)S(1)}, f32[130,1,256]{2,1,0:T(1,128)S(1)}, u32[]{:S(2)}, u32[]{:S(2)}) collective-permute-start(f32[130,1,256]{2,1,0:T(1,128)S(1)} %get-tuple-element.253), channel_id=1, source_target_pairs={{1,0},{2,1},{3,2},{0,3},{5,4},{6,5},{7,6},{4,7},{9,8},{10,9},{11,1... | collective-permute-start | bytes 399368 | tf_op jit(solution)/shard_map/ppermute | solution.py:20
  42.7 15.4 %fusion.254 = f32[128,16,256]{2,1,0:T(8,128)S(1)} fusion(f32[128,16,256]{2,1,0:T(8,128)S(1)} %bitcast.54, s32[]{:T(128)S(6)} %select_n.1227, s32[]{:T(128)S(6)} %select_n.1231, f32[1,16,256]{2,1,0:T(8,128)} %copy-done.2, f32[130,1,256]{2,1,0:T(1,128)} %collective-permute-done.3, f32[1,16,256]{2,1,0:T(8,128)} %copy-done.1, ...), kind=kLoop, calls=%fused_computation.525 | loop fusion | flops 26214400 | bytes 8688180 | tf_op jit(solution)/shard_map/add | solution.py:159
  63.6 3.6 collective-permute-start.6
  69.7 4.7 %collective-permute-done.7 = f32[130,1,256]{2,1,0:T(1,128)S(1)} collective-permute-done((f32[130,1,256]{2,1,0:T(1,128)S(1)}, f32[130,1,256]{2,1,0:T(1,128)S(1)}, u32[]{:S(2)}, u32[]{:S(2)}) %collective-permute-start.7) | collective-permute-done | bytes 133152 | tf_op jit(solution)/shard_map/ppermute | solution.py:17
  74.4 14.6 %fusion.229 = f32[128,16,256]{2,1,0:T(8,128)S(1)} fusion(f32[128,16,256]{2,1,0:T(8,128)S(1)} %fusion.254, s32[]{:T(128)S(6)} %select_n.1227, s32[]{:T(128)S(6)} %select_n.1231, f32[1,16,256]{2,1,0:T(8,128)S(1)} %collective-permute-done.4, f32[130,1,256]{2,1,0:T(1,128)S(1)} %collective-permute-done.7, f32[1,16,256]{2,1,0:T(8,128)S(1)} %collective-permute-done.5, ...), kind=kLoop, calls=%fused_computation.498 | loop fusion | flops 26214400 | bytes 8688180 | tf_op jit(solution)/shard_map/add | solution.py:159
  100.4 14.5 %fusion.204 = f32[128,16,256]{2,1,0:T(8,128)S(1)} fusion(f32[128,16,256]{2,1,0:T(8,128)S(1)} %fusion.229, s32[]{:T(128)S(6)} %select_n.1227, s32[]{:T(128)S(6)} %select_n.1231, f32[1,16,256]{2,1,0:T(8,128)S(1)} %collective-permute-done.8, f32[130,1,256]{2,1,0:T(1,128)S(1)} %collective-permute-done.11, f32[1,16,256]{2,1,0:T(8,128)S(1)} %collective-permute-done.9, ...), kind=kLoop, calls=%fused_computation.471 | loop fusion | flops 26214400 | bytes 8688180 | tf_op jit(solution)/shard_map/add | solution.py:159
  127.4 14.7 %fusion.179 = f32[128,16,256]{2,1,0:T(8,128)S(1)} fusion(f32[128,16,256]{2,1,0:T(8,128)S(1)} %fusion.204, s32[]{:T(128)S(6)} %select_n.1227, s32[]{:T(128)S(6)} %select_n.1231, f32[1,16,256]{2,1,0:T(8,128)S(1)} %collective-permute-done.12, f32[130,1,256]{2,1,0:T(1,128)S(1)} %collective-permute-done.15, f32[1,16,256]{2,1,0:T(8,128)S(1)} %collective-permute-done.13, ...), kind=kLoop, calls=%fused_computation.444 | loop fusion | flops 26214400 | bytes 8688180 | tf_op jit(solution)/shard_map/add | solution.py:159
  142.2 4.6 %add_select_fusion.23 = f32[128,16,256]{2,1,0:T(8,128)S(1)} fusion(f32[128,16,256]{2,1,0:T(8,128)S(1)} %fusion.179, s32[]{:T(128)S(6)} %select_n.1265, s32[]{:T(128)S(6)} %select_n.1259, s32[]{:T(128)S(6)} %select_n.1261, s32[]{:T(128)S(6)} %select_n.1263, pred[256]{0:T(512)(128)(4,1)S(1)} %copy-done.9, pred[256]{0:T(512)(128)(4,1)S(1)} %copy-done.10, ...), kind=kLoop, calls=%fused_computation.286 | loop fusion | flops 5242880 | bytes 4195088 | tf_op jit(solution)/shard_map/jit(_where)/select_n | solution.py:98
  146.8 4.5 %add_select_fusion.22 = f32[128,16,256]{2,1,0:T(8,128)S(1)} fusion(f32[128,16,256]{2,1,0:T(8,128)S(1)} %add_select_fusion.23, s32[]{:T(128)S(6)} %select_n.1273, s32[]{:T(128)S(6)} %select_n.1267, s32[]{:T(128)S(6)} %select_n.1269, s32[]{:T(128)S(6)} %select_n.1271, pred[256]{0:T(512)(128)(4,1)S(1)} %copy-done.19, pred[256]{0:T(512)(128)(4,1)S(1)} %copy-done.20, ...), kind=kLoop, calls=%fused_computation.285 | loop fusion | flops 5242880 | bytes 4195088 | tf_op jit(solution)/shard_map/jit(_where)/select_n | solution.py:98
  151.5 4.8 %add_select_fusion.21 = f32[128,16,256]{2,1,0:T(8,128)S(1)} fusion(f32[128,16,256]{2,1,0:T(8,128)S(1)} %add_select_fusion.22, s32[]{:T(128)S(6)} %select_n.1281, s32[]{:T(128)S(6)} %select_n.1275, s32[]{:T(128)S(6)} %select_n.1277, s32[]{:T(128)S(6)} %select_n.1279, pred[256]{0:T(512)(128)(4,1)S(1)} %copy-done.12, pred[256]{0:T(512)(128)(4,1)S(1)} %copy-done.13, ...), kind=kLoop, calls=%fused_computation.284 | loop fusion | flops 5242880 | bytes 4195088 | tf_op jit(solution)/shard_map/jit(_where)/select_n | solution.py:98
  156.4 4.6 %add_select_fusion.20 = f32[128,16,256]{2,1,0:T(8,128)S(1)} fusion(f32[128,16,256]{2,1,0:T(8,128)S(1)} %add_select_fusion.21, s32[]{:T(128)S(6)} %select_n.1289, s32[]{:T(128)S(6)} %select_n.1283, s32[]{:T(128)S(6)} %select_n.1285, s32[]{:T(128)S(6)} %select_n.1287, pred[256]{0:T(512)(128)(4,1)S(1)} %copy-done.15, pred[256]{0:T(512)(128)(4,1)S(1)} %copy-done.16, ...), kind=kLoop, calls=%fused_computation.283 | loop fusion | flops 5242880 | bytes 4195088 | tf_op jit(solution)/shard_map/jit(_where)/select_n | solution.py:98
  161.0 4.5 %add_select_fusion.19 = f32[128,16,256]{2,1,0:T(8,128)S(1)} fusion(f32[128,16,256]{2,1,0:T(8,128)S(1)} %add_select_fusion.20, s32[]{:T(128)S(6)} %select_n.1297, s32[]{:T(128)S(6)} %select_n.1291, s32[]{:T(128)S(6)} %select_n.1293, s32[]{:T(128)S(6)} %select_n.1295, pred[256]{0:T(512)(128)(4,1)S(1)} %copy-done.21, pred[256]{0:T(512)(128)(4,1)S(1)} %copy-done.22, ...), kind=kLoop, calls=%fused_computation.282 | loop fusion | flops 5242880 | bytes 4195088 | tf_op jit(solution)/shard_map/jit(_where)/select_n | solution.py:98
  165.6 5.0 %add_select_fusion.18 = f32[128,16,256]{2,1,0:T(8,128)S(1)} fusion(f32[128,16,256]{2,1,0:T(8,128)S(1)} %add_select_fusion.19, s32[]{:T(128)S(6)} %select_n.1305, s32[]{:T(128)S(6)} %select_n.1299, s32[]{:T(128)S(6)} %select_n.1301, s32[]{:T(128)S(6)} %select_n.1303, pred[256]{0:T(512)(128)(4,1)S(1)} %copy-done.24, pred[256]{0:T(512)(128)(4,1)S(1)} %copy-done.25, ...), kind=kLoop, calls=%fused_computation.281 | loop fusion | flops 5242880 | bytes 4195088 | tf_op jit(solution)/shard_map/jit(_where)/select_n | solution.py:98
  182.3 3.6 %fusion.22 = f32[128,16,256]{2,1,0:T(8,128)} fusion(f32[128,16,256]{2,1,0:T(8,128)S(1)} %add_select_fusion.13, s32[]{:T(128)S(6)} %select_n.1329, s32[]{:T(128)S(6)} %select_n.1327, f32[]{:T(128)} %bitcast.19, pred[256]{0:T(512)(128)(4,1)S(1)} %copy-done.31), kind=kLoop, calls=%fused_computation.287 | loop fusion | flops 3670016 | bytes 4194572 | tf_op jit(solution)/shard_map/mul | solution.py:173
  186.9 55.7 %all-gather.3.cloned.1.call-done = f32[512,16,256]{2,1,0:T(8,128)} async-done(((f32[128,16,256]{2,1,0:T(8,128)}), f32[512,16,256]{2,1,0:T(8,128)}) %all-gather.3.cloned.1.call-update) | async-done | bytes 8388624 | tf_op jit(solution)/shard_map/all_gather | solution.py:178
  242.6 63.3 %while.15 = (s32[]{:T(128)}, f32[128,16,256]{0,1,2:T(8,128)}, s32[4]{0:T(128)S(1)}, s32[4]{0:T(128)S(1)}, s32[256]{0:T(256)S(1)}, /*index=5*/f32[4,128,16,256]{3...) while((s32[]{:T(128)}, f32[128,16,256]{0,1,2:T(8,128)}, ...), condition=%wide.region_5.7_spmd.clone.clone, body=%wide.region_1.6_spmd.sunk.clone.clone.sunk | while | flops 2568969 | bytes 18895292 | solution.py:190
  254.5 2.6 bitcast_add_fusion.2
  269.2 4.2 %bitcast_add_fusion.2 = f32[128,16,256]{0,1,2:T(8,128)} fusion(f32[128,16,256]{0,1,2:T(8,128)} %get-tuple-element.368, f32[256,128,16]{1,2,0:T(8,128)S(1)} %gather_fusion, pred[256]{0:T(512)(128)(4,1)S(1)} %compare_reduce_fusion.2, pred[256]{0:T(512)(128)(4,1)S(1)} %compare_and_fusion.2, pred[]{:T(512)S(6)} %compare.116), kind=kLoop, calls=%fused_computation.2.clone.1 | loop fusion | flops 2097152 | bytes 6291969 | tf_op jit(solution)/shard_map/while/body/eval_jaxpr/add | solution.py:187
  285.4 4.2 %bitcast_add_fusion.2 = f32[128,16,256]{0,1,2:T(8,128)} fusion(f32[128,16,256]{0,1,2:T(8,128)} %get-tuple-element.368, f32[256,128,16]{1,2,0:T(8,128)S(1)} %gather_fusion, pred[256]{0:T(512)(128)(4,1)S(1)} %compare_reduce_fusion.2, pred[256]{0:T(512)(128)(4,1)S(1)} %compare_and_fusion.2, pred[]{:T(512)S(6)} %compare.116), kind=kLoop, calls=%fused_computation.2.clone.1 | loop fusion | flops 2097152 | bytes 6291969 | tf_op jit(solution)/shard_map/while/body/eval_jaxpr/add | solution.py:187
  301.6 4.2 %bitcast_add_fusion.2 = f32[128,16,256]{0,1,2:T(8,128)} fusion(f32[128,16,256]{0,1,2:T(8,128)} %get-tuple-element.368, f32[256,128,16]{1,2,0:T(8,128)S(1)} %gather_fusion, pred[256]{0:T(512)(128)(4,1)S(1)} %compare_reduce_fusion.2, pred[256]{0:T(512)(128)(4,1)S(1)} %compare_and_fusion.2, pred[]{:T(512)S(6)} %compare.116), kind=kLoop, calls=%fused_computation.2.clone.1 | loop fusion | flops 2097152 | bytes 6291969 | tf_op jit(solution)/shard_map/while/body/eval_jaxpr/add | solution.py:187
  305.8 3.4 copy.26
  309.2 6.1 %add_select_fusion.11 = f32[128,16,256]{2,1,0:T(8,128)S(1)} fusion(f32[128,16,256]{2,1,0:T(8,128)} %copy.26, s32[]{:T(128)S(6)} %select_n.1329, s32[]{:T(128)S(6)} %select_n.1327, pred[256]{0:T(512)(128)(4,1)S(1)} %copy-done.31), kind=kLoop, calls=%fused_computation.274 | loop fusion | flops 3145728 | bytes 4194568 | tf_op jit(solution)/shard_map/jit(_where)/select_n | solution.py:104
  324.3 2.7 add_select_fusion.6
  327.0 4.6 %add_select_fusion.5 = f32[128,16,256]{2,1,0:T(8,128)S(1)} fusion(f32[128,16,256]{2,1,0:T(8,128)S(1)} %add_select_fusion.6, s32[]{:T(128)S(6)} %select_n.1305, s32[]{:T(128)S(6)} %select_n.1299, s32[]{:T(128)S(6)} %select_n.1301, s32[]{:T(128)S(6)} %select_n.1303, pred[256]{0:T(512)(128)(4,1)S(1)} %copy-done.24, pred[256]{0:T(512)(128)(4,1)S(1)} %copy-done.25, ...), kind=kLoop, calls=%fused_computation.268 | loop fusion | flops 5242880 | bytes 4195088 | tf_op jit(solution)/shard_map/jit(_where)/select_n | solution.py:98
  331.6 4.5 %add_select_fusion.4 = f32[128,16,256]{2,1,0:T(8,128)S(1)} fusion(f32[128,16,256]{2,1,0:T(8,128)S(1)} %add_select_fusion.5, s32[]{:T(128)S(6)} %select_n.1297, s32[]{:T(128)S(6)} %select_n.1291, s32[]{:T(128)S(6)} %select_n.1293, s32[]{:T(128)S(6)} %select_n.1295, pred[256]{0:T(512)(128)(4,1)S(1)} %copy-done.21, pred[256]{0:T(512)(128)(4,1)S(1)} %copy-done.22, ...), kind=kLoop, calls=%fused_computation.267 | loop fusion | flops 5242880 | bytes 4195088 | tf_op jit(solution)/shard_map/jit(_where)/select_n | solution.py:98
  336.2 4.8 %add_select_fusion.3 = f32[128,16,256]{2,1,0:T(8,128)S(1)} fusion(f32[128,16,256]{2,1,0:T(8,128)S(1)} %add_select_fusion.4, s32[]{:T(128)S(6)} %select_n.1289, s32[]{:T(128)S(6)} %select_n.1283, s32[]{:T(128)S(6)} %select_n.1285, s32[]{:T(128)S(6)} %select_n.1287, pred[256]{0:T(512)(128)(4,1)S(1)} %copy-done.15, pred[256]{0:T(512)(128)(4,1)S(1)} %copy-done.16, ...), kind=kLoop, calls=%fused_computation.266 | loop fusion | flops 5242880 | bytes 4195088 | tf_op jit(solution)/shard_map/jit(_where)/select_n | solution.py:98
  341.0 4.5 %add_select_fusion.2 = f32[128,16,256]{2,1,0:T(8,128)S(1)} fusion(f32[128,16,256]{2,1,0:T(8,128)S(1)} %add_select_fusion.3, s32[]{:T(128)S(6)} %select_n.1281, s32[]{:T(128)S(6)} %select_n.1275, s32[]{:T(128)S(6)} %select_n.1277, s32[]{:T(128)S(6)} %select_n.1279, pred[256]{0:T(512)(128)(4,1)S(1)} %copy-done.12, pred[256]{0:T(512)(128)(4,1)S(1)} %copy-done.13, ...), kind=kLoop, calls=%fused_computation.265 | loop fusion | flops 5242880 | bytes 4195088 | tf_op jit(solution)/shard_map/jit(_where)/select_n | solution.py:98
  345.5 4.8 %add_select_fusion.1 = f32[128,16,256]{2,1,0:T(8,128)S(1)} fusion(f32[128,16,256]{2,1,0:T(8,128)S(1)} %add_select_fusion.2, s32[]{:T(128)S(6)} %select_n.1273, s32[]{:T(128)S(6)} %select_n.1267, s32[]{:T(128)S(6)} %select_n.1269, s32[]{:T(128)S(6)} %select_n.1271, pred[256]{0:T(512)(128)(4,1)S(1)} %copy-done.19, pred[256]{0:T(512)(128)(4,1)S(1)} %copy-done.20, ...), kind=kLoop, calls=%fused_computation.264 | loop fusion | flops 5242880 | bytes 4195088 | tf_op jit(solution)/shard_map/jit(_where)/select_n | solution.py:98
  350.3 5.8 %fusion.23 = f32[1,128,16,256]{3,2,1,0:T(8,128)} fusion(f32[128,16,256]{2,1,0:T(8,128)S(1)} %add_select_fusion.1, s32[]{:T(128)S(6)} %select_n.1265, s32[]{:T(128)S(6)} %select_n.1259, s32[]{:T(128)S(6)} %select_n.1261, s32[]{:T(128)S(6)} %select_n.1263, pred[256]{0:T(512)(128)(4,1)S(1)} %copy-done.9, pred[256]{0:T(512)(128)(4,1)S(1)} %copy-done.10, ...), kind=kLoop, calls=%fused_computation.288 | loop fusion | flops 5242880 | bytes 4195088 | tf_op jit(solution)/shard_map/broadcast_in_dim | solution.py:191
  (193 shorter events, 103.7 us)
Async XLA Ops:
  6.5 236.0 %all-gather.3.cloned.1.call-start = ((), (), s32[]{:S(2)}) async-start(), calls=%async_computation | async-start | bytes 10485760 | tf_op jit(solution)/shard_map/all_gather | solution.py:178
  7.3 23.8 %collective-permute-start.1 = (f32[1,16,256]{2,1,0:T(8,128)S(1)}, f32[1,16,256]{2,1,0:T(8,128)S(1)}, u32[]{:S(2)}, u32[]{:S(2)}) collective-permute-start(f32[1,16,256]{2,1,0:T(8,128)S(1)} %get-tuple-element.277), channel_id=1, source_target_pairs={{0,4},{4,0},{1,5},{5,1},{2,6},{6,2},{3,7},{7,3},{8,12},{12,8},{9,1... | collective-permute-start | bytes 49160 | tf_op jit(solution)/shard_map/ppermute | solution.py:17
  10.2 20.8 %collective-permute-start = (f32[1,16,256]{2,1,0:T(8,128)S(1)}, f32[1,16,256]{2,1,0:T(8,128)S(1)}, u32[]{:S(2)}, u32[]{:S(2)}) collective-permute-start(f32[1,16,256]{2,1,0:T(8,128)S(1)} %get-tuple-element.278), channel_id=1, source_target_pairs={{4,0},{0,4},{5,1},{1,5},{6,2},{2,6},{7,3},{3,7},{12,8},{8,12},{13,... | collective-permute-start | bytes 49160 | tf_op jit(solution)/shard_map/ppermute | solution.py:20
  15.1 12.2 %copy-start.6 = (s32[256]{0:T(256)}, s32[256]{0:T(256)S(1)}, u32[]{:S(2)}) copy-start(s32[256]{0:T(256)S(1)} %get-tuple-element.244) | copy-start | bytes 3076
  18.1 9.8 %copy-start.32 = (f32[2,4]{1,0:T(2,128)S(1)}, f32[2,4]{1,0:T(2,128)}, u32[]{:S(2)}) copy-start(f32[2,4]{1,0:T(2,128)} %param.13) | copy-start | bytes 100
  31.7 10.7 %collective-permute-start.2 = (f32[130,1,256]{2,1,0:T(1,128)S(1)}, f32[130,1,256]{2,1,0:T(1,128)S(1)}, u32[]{:S(2)}, u32[]{:S(2)}) collective-permute-start(f32[130,1,256]{2,1,0:T(1,128)S(1)} %get-tuple-element.253), channel_id=1, source_target_pairs={{1,0},{2,1},{3,2},{0,3},{5,4},{6,5},{7,6},{4,7},{9,8},{10,9},{11,1... | collective-permute-start | bytes 399368 | tf_op jit(solution)/shard_map/ppermute | solution.py:20
  35.8 6.9 %collective-permute-start.3 = (f32[130,1,256]{2,1,0:T(1,128)S(1)}, f32[130,1,256]{2,1,0:T(1,128)}, u32[]{:S(2)}, u32[]{:S(2)}) collective-permute-start(f32[130,1,256]{2,1,0:T(1,128)S(1)} %get-tuple-element.254), channel_id=1, source_target_pairs={{0,1},{1,2},{2,3},{3,0},{4,5},{5,6},{6,7},{7,4},{8,9},{9,10},{10,1... | collective-permute-start | bytes 399368 | tf_op jit(solution)/shard_map/ppermute | solution.py:17
  58.1 3.8 %collective-permute-start.5 = (f32[1,16,256]{2,1,0:T(8,128)S(1)}, f32[1,16,256]{2,1,0:T(8,128)S(1)}, u32[]{:S(2)}, u32[]{:S(2)}) collective-permute-start(f32[1,16,256]{2,1,0:T(8,128)S(1)} %get-tuple-element.271), channel_id=1, source_target_pairs={{0,4},{4,0},{1,5},{5,1},{2,6},{6,2},{3,7},{7,3},{8,12},{12,8},{9,1... | collective-permute-start | bytes 49160 | tf_op jit(solution)/shard_map/ppermute | solution.py:17
  59.6 3.7 %collective-permute-start.4 = (f32[1,16,256]{2,1,0:T(8,128)S(1)}, f32[1,16,256]{2,1,0:T(8,128)S(1)}, u32[]{:S(2)}, u32[]{:S(2)}) collective-permute-start(f32[1,16,256]{2,1,0:T(8,128)S(1)} %get-tuple-element.272), channel_id=1, source_target_pairs={{4,0},{0,4},{5,1},{1,5},{6,2},{2,6},{7,3},{3,7},{12,8},{8,12},{13,... | collective-permute-start | bytes 49160 | tf_op jit(solution)/shard_map/ppermute | solution.py:20
  63.6 6.1 %collective-permute-start.6 = (f32[130,1,256]{2,1,0:T(1,128)S(1)}, f32[130,1,256]{2,1,0:T(1,128)S(1)}, u32[]{:S(2)}, u32[]{:S(2)}) collective-permute-start(f32[130,1,256]{2,1,0:T(1,128)S(1)} %get-tuple-element.251), channel_id=1, source_target_pairs={{1,0},{2,1},{3,2},{0,3},{5,4},{6,5},{7,6},{4,7},{9,8},{10,9},{11,1... | collective-permute-start | bytes 399368 | tf_op jit(solution)/shard_map/ppermute | solution.py:20
  67.2 7.2 %copy-start.4 = (pred[256]{0:T(512)(128)(4,1)S(1)}, pred[256]{0:T(512)(128)(4,1)}, u32[]{:S(2)}) copy-start(pred[256]{0:T(512)(128)(4,1)} %get-tuple-element.311) | copy-start | bytes 772
  67.2 7.2 %copy-start.5 = (pred[256]{0:T(512)(128)(4,1)S(1)}, pred[256]{0:T(512)(128)(4,1)}, u32[]{:S(2)}) copy-start(pred[256]{0:T(512)(128)(4,1)} %get-tuple-element.312) | copy-start | bytes 772
  67.2 7.2 %collective-permute-start.7 = (f32[130,1,256]{2,1,0:T(1,128)S(1)}, f32[130,1,256]{2,1,0:T(1,128)S(1)}, u32[]{:S(2)}, u32[]{:S(2)}) collective-permute-start(f32[130,1,256]{2,1,0:T(1,128)S(1)} %get-tuple-element.252), channel_id=1, source_target_pairs={{0,1},{1,2},{2,3},{3,0},{4,5},{5,6},{6,7},{7,4},{8,9},{9,10},{10,1... | collective-permute-start | bytes 399368 | tf_op jit(solution)/shard_map/ppermute | solution.py:17
  89.0 3.8 %collective-permute-start.9 = (f32[1,16,256]{2,1,0:T(8,128)S(1)}, f32[1,16,256]{2,1,0:T(8,128)S(1)}, u32[]{:S(2)}, u32[]{:S(2)}) collective-permute-start(f32[1,16,256]{2,1,0:T(8,128)S(1)} %get-tuple-element.265), channel_id=1, source_target_pairs={{0,4},{4,0},{1,5},{5,1},{2,6},{6,2},{3,7},{7,3},{8,12},{12,8},{9,1... | collective-permute-start | bytes 49160 | tf_op jit(solution)/shard_map/ppermute | solution.py:17
  89.6 3.7 %collective-permute-start.8 = (f32[1,16,256]{2,1,0:T(8,128)S(1)}, f32[1,16,256]{2,1,0:T(8,128)S(1)}, u32[]{:S(2)}, u32[]{:S(2)}) collective-permute-start(f32[1,16,256]{2,1,0:T(8,128)S(1)} %get-tuple-element.266), channel_id=1, source_target_pairs={{4,0},{0,4},{5,1},{1,5},{6,2},{2,6},{7,3},{3,7},{12,8},{8,12},{13,... | collective-permute-start | bytes 49160 | tf_op jit(solution)/shard_map/ppermute | solution.py:20
  93.5 5.0 %collective-permute-start.10 = (f32[130,1,256]{2,1,0:T(1,128)S(1)}, f32[130,1,256]{2,1,0:T(1,128)S(1)}, u32[]{:S(2)}, u32[]{:S(2)}) collective-permute-start(f32[130,1,256]{2,1,0:T(1,128)S(1)} %get-tuple-element.249), channel_id=1, source_target_pairs={{1,0},{2,1},{3,2},{0,3},{5,4},{6,5},{7,6},{4,7},{9,8},{10,9},{11,1... | collective-permute-start | bytes 399368 | tf_op jit(solution)/shard_map/ppermute | solution.py:20
  93.6 6.8 %collective-permute-start.11 = (f32[130,1,256]{2,1,0:T(1,128)S(1)}, f32[130,1,256]{2,1,0:T(1,128)S(1)}, u32[]{:S(2)}, u32[]{:S(2)}) collective-permute-start(f32[130,1,256]{2,1,0:T(1,128)S(1)} %get-tuple-element.250), channel_id=1, source_target_pairs={{0,1},{1,2},{2,3},{3,0},{4,5},{5,6},{6,7},{7,4},{8,9},{9,10},{10,1... | collective-permute-start | bytes 399368 | tf_op jit(solution)/shard_map/ppermute | solution.py:17
  115.0 3.8 %collective-permute-start.13 = (f32[1,16,256]{2,1,0:T(8,128)S(1)}, f32[1,16,256]{2,1,0:T(8,128)S(1)}, u32[]{:S(2)}, u32[]{:S(2)}) collective-permute-start(f32[1,16,256]{2,1,0:T(8,128)S(1)} %get-tuple-element.259), channel_id=1, source_target_pairs={{0,4},{4,0},{1,5},{5,1},{2,6},{6,2},{3,7},{7,3},{8,12},{12,8},{9,1... | collective-permute-start | bytes 49160 | tf_op jit(solution)/shard_map/ppermute | solution.py:17
  116.5 3.7 %collective-permute-start.12 = (f32[1,16,256]{2,1,0:T(8,128)S(1)}, f32[1,16,256]{2,1,0:T(8,128)S(1)}, u32[]{:S(2)}, u32[]{:S(2)}) collective-permute-start(f32[1,16,256]{2,1,0:T(8,128)S(1)} %get-tuple-element.260), channel_id=1, source_target_pairs={{4,0},{0,4},{5,1},{1,5},{6,2},{2,6},{7,3},{3,7},{12,8},{8,12},{13,... | collective-permute-start | bytes 49160 | tf_op jit(solution)/shard_map/ppermute | solution.py:20
  120.5 5.0 %collective-permute-start.14 = (f32[130,1,256]{2,1,0:T(1,128)S(1)}, f32[130,1,256]{2,1,0:T(1,128)S(1)}, u32[]{:S(2)}, u32[]{:S(2)}) collective-permute-start(f32[130,1,256]{2,1,0:T(1,128)S(1)} %get-tuple-element.247), channel_id=1, source_target_pairs={{1,0},{2,1},{3,2},{0,3},{5,4},{6,5},{7,6},{4,7},{9,8},{10,9},{11,1... | collective-permute-start | bytes 399368 | tf_op jit(solution)/shard_map/ppermute | solution.py:20
  120.6 6.8 %collective-permute-start.15 = (f32[130,1,256]{2,1,0:T(1,128)S(1)}, f32[130,1,256]{2,1,0:T(1,128)S(1)}, u32[]{:S(2)}, u32[]{:S(2)}) collective-permute-start(f32[130,1,256]{2,1,0:T(1,128)S(1)} %get-tuple-element.248), channel_id=1, source_target_pairs={{0,1},{1,2},{2,3},{3,0},{4,5},{5,6},{6,7},{7,4},{8,9},{9,10},{10,1... | collective-permute-start | bytes 399368 | tf_op jit(solution)/shard_map/ppermute | solution.py:17
  127.4 14.7 %copy-start.9 = (pred[256]{0:T(512)(128)(4,1)S(1)}, pred[256]{0:T(512)(128)(4,1)}, u32[]{:S(2)}) copy-start(pred[256]{0:T(512)(128)(4,1)} %get-tuple-element.309) | copy-start | bytes 772
  127.4 14.7 %copy-start.10 = (pred[256]{0:T(512)(128)(4,1)S(1)}, pred[256]{0:T(512)(128)(4,1)}, u32[]{:S(2)}) copy-start(pred[256]{0:T(512)(128)(4,1)} %get-tuple-element.310) | copy-start | bytes 772
  127.4 14.8 %copy-start.11 = (pred[256]{0:T(512)(128)(4,1)S(1)}, pred[256]{0:T(512)(128)(4,1)}, u32[]{:S(2)}) copy-start(pred[256]{0:T(512)(128)(4,1)} %get-tuple-element.290) | copy-start | bytes 772
  151.4 4.9 %copy-start.15 = (pred[256]{0:T(512)(128)(4,1)S(1)}, pred[256]{0:T(512)(128)(4,1)}, u32[]{:S(2)}) copy-start(pred[256]{0:T(512)(128)(4,1)} %get-tuple-element.303) | copy-start | bytes 772
  151.4 4.9 %copy-start.16 = (pred[256]{0:T(512)(128)(4,1)S(1)}, pred[256]{0:T(512)(128)(4,1)}, u32[]{:S(2)}) copy-start(pred[256]{0:T(512)(128)(4,1)} %get-tuple-element.304) | copy-start | bytes 772
  151.5 4.9 %copy-start.18 = (pred[256]{0:T(512)(128)(4,1)S(1)}, pred[256]{0:T(512)(128)(4,1)}, u32[]{:S(2)}) copy-start(pred[256]{0:T(512)(128)(4,1)} %get-tuple-element.287) | copy-start | bytes 772
  156.3 4.7 %copy-start.21 = (pred[256]{0:T(512)(128)(4,1)S(1)}, pred[256]{0:T(512)(128)(4,1)}, u32[]{:S(2)}) copy-start(pred[256]{0:T(512)(128)(4,1)} %get-tuple-element.301) | copy-start | bytes 772
  156.3 4.7 %copy-start.22 = (pred[256]{0:T(512)(128)(4,1)S(1)}, pred[256]{0:T(512)(128)(4,1)}, u32[]{:S(2)}) copy-start(pred[256]{0:T(512)(128)(4,1)} %get-tuple-element.302) | copy-start | bytes 772
  156.3 4.7 %copy-start.23 = (pred[256]{0:T(512)(128)(4,1)S(1)}, pred[256]{0:T(512)(128)(4,1)}, u32[]{:S(2)}) copy-start(pred[256]{0:T(512)(128)(4,1)} %get-tuple-element.286) | copy-start | bytes 772
  165.6 5.0 %copy-start.26 = (pred[256]{0:T(512)(128)(4,1)S(1)}, pred[256]{0:T(512)(128)(4,1)}, u32[]{:S(2)}) copy-start(pred[256]{0:T(512)(128)(4,1)} %get-tuple-element.285) | copy-start | bytes 772
  186.0 56.6 %copy-start.33 = (s32[4]{0:T(128)S(1)}, s32[4]{0:T(128)}, u32[]{:S(2)}) copy-start(s32[4]{0:T(128)} %param.11) | copy-start | bytes 52
  (19 other events, 58.6 us)
Sparse Core Ops, SparseCore 0:
  186.1 56.3 all-gather.2
where the time goes:
time: 370 us; the launch traced here: 363 us
  other arithmetic  180 us (49%)
  waiting for transfers between devices  77.8 us (21%)
  local copies, waits for them, and re-layouts  49 us (13%)
  between operations  23.9 us (6%)
  starting transfers between devices  21.6 us (6%)
  loops' own time  11.2 us (3%)
    add x4, other arithmetic, advance(): return centre + change + rate * centre / (1.0 + centre * centre)  59.2 us
    all_gather x1, waiting for transfers between devices, local(): piece = lax.all_gather(surplus[None], 'comp', axis=0, tiled=True)  55.7 us
    select_n x11, other arithmetic, fourth_pass(): jnp.where(depth_fourth == level, values + factor * (ahead + behind), values)  51.5 us
    select_n x11, other arithmetic, third_pass(): jnp.where(depth_third == level, values + factor * (ahead + behind), values)  29.3 us
    dynamic_slice x12, local copies, waits for them, and re-layouts, local(): carry, unused = lax.scan(add_grid, carry, (piece, sources))  18.7 us
    add x4, other arithmetic, add_grid(): inner + jnp.where(found, jnp.take(remote, source, axis=-1), 0.0)  15.3 us
    ppermute x8, waiting for transfers between devices, extended(): lax.ppermute(lax.slice_in_dim(block, block.shape[dim] - width, None, axis...  11.6 us
    another operation x1, loops' own time, local(): carry, unused = lax.scan(add_grid, carry, (piece, sources))  11.2 us
  transfers between devices with their start and end apart: 17, of which 14 were waited for; matrix products, arithmetic and copies ran while one was open for 6% of the time, Pallas kernels for 0%

commit v1 on v0

--- a/solution.py
+++ b/solution.py
@@ -175,7 +175,22 @@
     own_slots = slot_positions(level_a, table)
     columns = jnp.arange(size, dtype=jnp.int32)
     carry = jnp.zeros_like(surplus)
-    piece = lax.all_gather(surplus[None], "comp", axis=0, tiled=True)
+    ways, here, step = (lax.axis_size("comp"), lax.axis_index("comp"), surplus[None].shape[0])
+    shape = [n * ways if d == 0 else n for d, n in enumerate(surplus[None].shape)]
+    piece = lax.dynamic_update_slice_in_dim(
+        jnp.zeros(shape, surplus[None].dtype), surplus[None], here * step, axis=0
+    )
+    going_up = going_down = surplus[None]
+    for far in range(1, ways // 2 + 1):
+        going_up = lax.ppermute(going_up, "comp", [(d, (d + 1) % ways) for d in range(ways)])
+        piece = lax.dynamic_update_slice_in_dim(piece, going_up, (here - far) % ways * step, axis=0)
+        if 2 * far < ways:
+            going_down = lax.ppermute(
+                going_down, "comp", [(d, (d - 1) % ways) for d in range(ways)]
+            )
+            piece = lax.dynamic_update_slice_in_dim(
+                piece, going_down, (here + far) % ways * step, axis=0
+            )
 
     def add_grid(inner, item):
         remote, source_grid = item

time: 370 us -> 365 us (0.986)
  local copies, waits for them, and re-layouts: 49 us -> 65.3 us
  between operations: 23.9 us -> 11.2 us
  other arithmetic: 180 us -> 175 us
  waiting for transfers between devices: 77.8 us -> 73.3 us
    all_gather x1 -> x0, waiting for transfers between devices: 55.7 us -> none  [local(): piece = lax.all_gather(surplus[None], 'comp', axis=0, tiled=True)]
    ppermute x0 -> x3, waiting for transfers between devices: none -> 51.5 us  [the longest x2 51.5 us: local(): lax.ppermute(going_up, 'comp', [(d, (d + 1) % ways) for d in range(ways)])]
    dynamic_slice x12 -> x4, local copies, waits for them, and re-layouts: 18.7 us -> 2.3 us  [local(): carry, unused = lax.scan(add_grid, carry, (piece, sources))]
    squeeze x0 -> x4, local copies, waits for them, and re-layouts: none -> 12.1 us  [local(): carry, unused = lax.scan(add_grid, carry, (piece, sources))]
    ppermute x0 -> x3, local copies, waits for them, and re-layouts: none -> 9.33 us  [the longest x2 5.85 us: local(): lax.ppermute(going_up, 'comp', [(d, (d + 1) % ways) for d in range(ways)])]
    broadcast_in_dim x0 -> x2, local copies, waits for them, and re-layouts: none -> 6.32 us  [the longest x1 4.05 us: local(): jnp.zeros(shape, surplus[None].dtype)]
    dynamic_update_slice x0 -> x4, local copies, waits for them, and re-layouts: none -> 5.94 us  [the longest x2 3.01 us: local(): lax.dynamic_update_slice_in_dim(piece, going_up, (here - far) % ways * st...]
    ppermute x8, starting transfers between devices: 10.5 us -> 14.8 us  [extended(): lax.ppermute(lax.slice_in_dim(block, 0, width, axis=dim), axis, backward)]
  transfers between devices with their start and end apart: 17 -> 19, of which waited for: 14 -> 14; matrix products, arithmetic and copies ran while one was open for 6% -> 11% of each run, Pallas kernels for 0% -> 0%
where the time goes in v1:
time: 365 us; the launch traced here: 357 us
  other arithmetic  175 us (48%)
  waiting for transfers between devices  73.3 us (20%)
  local copies, waits for them, and re-layouts  65.3 us (18%)
  starting transfers between devices  23.7 us (6%)
  between operations  11.2 us (3%)
  loops' own time  9.14 us (3%)
    add x4, other arithmetic, advance(): return centre + change + rate * centre / (1.0 + centre * centre)  59.7 us
    select_n x11, other arithmetic, fourth_pass(): jnp.where(depth_fourth == level, values + factor * (ahead + behind), values)  51.8 us
    ppermute x2, waiting for transfers between devices, local(): lax.ppermute(going_up, 'comp', [(d, (d + 1) % ways) for d in range(ways)])  51.5 us
    select_n x11, other arithmetic, third_pass(): jnp.where(depth_third == level, values + factor * (ahead + behind), values)  25.5 us
    add x4, other arithmetic, add_grid(): inner + jnp.where(found, jnp.take(remote, source, axis=-1), 0.0)  15.4 us
    ppermute x8, starting transfers between devices, extended(): lax.ppermute(lax.slice_in_dim(block, 0, width, axis=dim), axis, backward)  14.8 us
    squeeze x4, local copies, waits for them, and re-layouts, local(): carry, unused = lax.scan(add_grid, carry, (piece, sources))  12.1 us
    ppermute x8, waiting for transfers between devices, extended(): lax.ppermute(lax.slice_in_dim(block, block.shape[dim] - width, None, axis...  11.9 us
  transfers between devices with their start and end apart: 19, of which 14 were waited for; matrix products, arithmetic and copies ran while one was open for 11% of the time, Pallas kernels for 0%

profile of v1, /device:TPU:0, one launch (start us, length us, event | category | flops | bytes accessed | tf_op | source)
XLA Modules:
  0.0 357.4 jit_solution(13435996965488043734)
XLA Ops:
  3.7 5.1 %fusion.316 = (f32[128,16,255]{2,1,0:T(8,128)}, f32[128,16,255]{2,1,0:T(8,128)}) fusion(f32[128,16,256]{2,1,0:T(8,128)} %bitcast.52), kind=kLoop, calls=%fused_computation.727 | loop fusion | bytes 8355840 | tf_op jit(solution)/shard_map/jit(_roll_static)/slice | solution.py:81
  24.0 4.1 %collective-permute-start.2 = (f32[130,1,256]{2,1,0:T(1,128)S(1)}, f32[130,1,256]{2,1,0:T(1,128)S(1)}, u32[]{:S(2)}, u32[]{:S(2)}) collective-permute-start(f32[130,1,256]{2,1,0:T(1,128)S(1)} %get-tuple-element.235), channel_id=1, source_target_pairs={{1,0},{2,1},{3,2},{0,3},{5,4},{6,5},{7,6},{4,7},{9,8},{10,9},{11,1... | collective-permute-start | bytes 399368 | tf_op jit(solution)/shard_map/ppermute | solution.py:20
  36.4 15.5 %fusion.255 = f32[128,16,256]{2,1,0:T(8,128)S(1)} fusion(f32[128,16,256]{2,1,0:T(8,128)S(1)} %bitcast.55, s32[]{:T(128)S(6)} %select_n.1257, s32[]{:T(128)S(6)} %select_n.1261, f32[1,16,256]{2,1,0:T(8,128)} %copy-done.4, f32[130,1,256]{2,1,0:T(1,128)} %collective-permute-done.3, f32[1,16,256]{2,1,0:T(8,128)} %copy-done.5, ...), kind=kLoop, calls=%fused_computation.526 | loop fusion | flops 26214400 | bytes 8688180 | tf_op jit(solution)/shard_map/add | solution.py:159
  57.4 3.9 %collective-permute-start.6 = (f32[130,1,256]{2,1,0:T(1,128)S(1)}, f32[130,1,256]{2,1,0:T(1,128)S(1)}, u32[]{:S(2)}, u32[]{:S(2)}) collective-permute-start(f32[130,1,256]{2,1,0:T(1,128)S(1)} %get-tuple-element.233), channel_id=1, source_target_pairs={{1,0},{2,1},{3,2},{0,3},{5,4},{6,5},{7,6},{4,7},{9,8},{10,9},{11,1... | collective-permute-start | bytes 399368 | tf_op jit(solution)/shard_map/ppermute | solution.py:20
  63.8 4.7 %collective-permute-done.7 = f32[130,1,256]{2,1,0:T(1,128)S(1)} collective-permute-done((f32[130,1,256]{2,1,0:T(1,128)S(1)}, f32[130,1,256]{2,1,0:T(1,128)S(1)}, u32[]{:S(2)}, u32[]{:S(2)}) %collective-permute-start.7) | collective-permute-done | bytes 133152 | tf_op jit(solution)/shard_map/ppermute | solution.py:17
  68.5 14.7 %fusion.230 = f32[128,16,256]{2,1,0:T(8,128)S(1)} fusion(f32[128,16,256]{2,1,0:T(8,128)S(1)} %fusion.255, s32[]{:T(128)S(6)} %select_n.1257, s32[]{:T(128)S(6)} %select_n.1261, f32[1,16,256]{2,1,0:T(8,128)S(1)} %collective-permute-done.4, f32[130,1,256]{2,1,0:T(1,128)S(1)} %collective-permute-done.7, f32[1,16,256]{2,1,0:T(8,128)S(1)} %collective-permute-done.5, ...), kind=kLoop, calls=%fused_computation.499 | loop fusion | flops 26214400 | bytes 8688180 | tf_op jit(solution)/shard_map/add | solution.py:159
  94.7 14.7 %fusion.205 = f32[128,16,256]{2,1,0:T(8,128)S(1)} fusion(f32[128,16,256]{2,1,0:T(8,128)S(1)} %fusion.230, s32[]{:T(128)S(6)} %select_n.1257, s32[]{:T(128)S(6)} %select_n.1261, f32[1,16,256]{2,1,0:T(8,128)S(1)} %collective-permute-done.8, f32[130,1,256]{2,1,0:T(1,128)S(1)} %collective-permute-done.11, f32[1,16,256]{2,1,0:T(8,128)S(1)} %collective-permute-done.9, ...), kind=kLoop, calls=%fused_computation.472 | loop fusion | flops 26214400 | bytes 8688180 | tf_op jit(solution)/shard_map/add | solution.py:159
  121.8 14.9 %fusion.180 = f32[128,16,256]{2,1,0:T(8,128)S(1)} fusion(f32[128,16,256]{2,1,0:T(8,128)S(1)} %fusion.205, s32[]{:T(128)S(6)} %select_n.1257, s32[]{:T(128)S(6)} %select_n.1261, f32[1,16,256]{2,1,0:T(8,128)S(1)} %collective-permute-done.12, f32[130,1,256]{2,1,0:T(1,128)S(1)} %collective-permute-done.15, f32[1,16,256]{2,1,0:T(8,128)S(1)} %collective-permute-done.13, ...), kind=kLoop, calls=%fused_computation.445 | loop fusion | flops 26214400 | bytes 8688180 | tf_op jit(solution)/shard_map/add | solution.py:159
  136.7 4.6 %add_select_fusion.23 = f32[128,16,256]{2,1,0:T(8,128)S(1)} fusion(f32[128,16,256]{2,1,0:T(8,128)S(1)} %fusion.180, s32[]{:T(128)S(6)} %select_n.1295, s32[]{:T(128)S(6)} %select_n.1289, s32[]{:T(128)S(6)} %select_n.1291, s32[]{:T(128)S(6)} %select_n.1293, pred[256]{0:T(512)(128)(4,1)S(1)} %copy-done.12, pred[256]{0:T(512)(128)(4,1)S(1)} %copy-done.13, ...), kind=kLoop, calls=%fused_computation.286 | loop fusion | flops 5242880 | bytes 4195088 | tf_op jit(solution)/shard_map/jit(_where)/select_n | solution.py:98
  141.4 4.6 %add_select_fusion.22 = f32[128,16,256]{2,1,0:T(8,128)S(1)} fusion(f32[128,16,256]{2,1,0:T(8,128)S(1)} %add_select_fusion.23, s32[]{:T(128)S(6)} %select_n.1303, s32[]{:T(128)S(6)} %select_n.1297, s32[]{:T(128)S(6)} %select_n.1299, s32[]{:T(128)S(6)} %select_n.1301, pred[256]{0:T(512)(128)(4,1)S(1)} %copy-done.17, pred[256]{0:T(512)(128)(4,1)S(1)} %copy-done.18, ...), kind=kLoop, calls=%fused_computation.285 | loop fusion | flops 5242880 | bytes 4195088 | tf_op jit(solution)/shard_map/jit(_where)/select_n | solution.py:98
  146.1 4.8 %add_select_fusion.21 = f32[128,16,256]{2,1,0:T(8,128)S(1)} fusion(f32[128,16,256]{2,1,0:T(8,128)S(1)} %add_select_fusion.22, s32[]{:T(128)S(6)} %select_n.1311, s32[]{:T(128)S(6)} %select_n.1305, s32[]{:T(128)S(6)} %select_n.1307, s32[]{:T(128)S(6)} %select_n.1309, pred[256]{0:T(512)(128)(4,1)S(1)} %copy-done.21, pred[256]{0:T(512)(128)(4,1)S(1)} %copy-done.22, ...), kind=kLoop, calls=%fused_computation.284 | loop fusion | flops 5242880 | bytes 4195088 | tf_op jit(solution)/shard_map/jit(_where)/select_n | solution.py:98
  151.0 4.6 %add_select_fusion.20 = f32[128,16,256]{2,1,0:T(8,128)S(1)} fusion(f32[128,16,256]{2,1,0:T(8,128)S(1)} %add_select_fusion.21, s32[]{:T(128)S(6)} %select_n.1319, s32[]{:T(128)S(6)} %select_n.1313, s32[]{:T(128)S(6)} %select_n.1315, s32[]{:T(128)S(6)} %select_n.1317, pred[256]{0:T(512)(128)(4,1)S(1)} %copy-done.23, pred[256]{0:T(512)(128)(4,1)S(1)} %copy-done.24, ...), kind=kLoop, calls=%fused_computation.283 | loop fusion | flops 5242880 | bytes 4195088 | tf_op jit(solution)/shard_map/jit(_where)/select_n | solution.py:98
  155.6 4.6 %add_select_fusion.19 = f32[128,16,256]{2,1,0:T(8,128)S(1)} fusion(f32[128,16,256]{2,1,0:T(8,128)S(1)} %add_select_fusion.20, s32[]{:T(128)S(6)} %select_n.1327, s32[]{:T(128)S(6)} %select_n.1321, s32[]{:T(128)S(6)} %select_n.1323, s32[]{:T(128)S(6)} %select_n.1325, pred[256]{0:T(512)(128)(4,1)S(1)} %copy-done.25, pred[256]{0:T(512)(128)(4,1)S(1)} %copy-done.26, ...), kind=kLoop, calls=%fused_computation.282 | loop fusion | flops 5242880 | bytes 4195088 | tf_op jit(solution)/shard_map/jit(_where)/select_n | solution.py:98
  160.3 5.0 %add_select_fusion.18 = f32[128,16,256]{2,1,0:T(8,128)S(1)} fusion(f32[128,16,256]{2,1,0:T(8,128)S(1)} %add_select_fusion.19, s32[]{:T(128)S(6)} %select_n.1335, s32[]{:T(128)S(6)} %select_n.1329, s32[]{:T(128)S(6)} %select_n.1331, s32[]{:T(128)S(6)} %select_n.1333, pred[256]{0:T(512)(128)(4,1)S(1)} %copy-done.29, pred[256]{0:T(512)(128)(4,1)S(1)} %copy-done.30, ...), kind=kLoop, calls=%fused_computation.281 | loop fusion | flops 5242880 | bytes 4195088 | tf_op jit(solution)/shard_map/jit(_where)/select_n | solution.py:98
  181.1 44.5 %collective-permute-done.16 = f32[1,128,16,256]{3,2,1,0:T(8,128)} collective-permute-done((f32[1,128,16,256]{3,2,1,0:T(8,128)S(1)}, f32[1,128,16,256]{3,2,1,0:T(8,128)}, u32[]{:S(2)}, u32[]{:S(2)}) %collective-permute-start.16) | collective-permute-done | bytes 2097184 | tf_op jit(solution)/shard_map/ppermute | solution.py:185
  228.2 4.0 %broadcast_in_dim.243 = f32[4,128,16,256]{1,2,3,0:T(8,128)} broadcast(f32[]{:T(128)} %constant.615.clone.1), dimensions={} | broadcast | bytes 8388612 | tf_op jit(solution)/shard_map/broadcast_in_dim | solution.py:181
  233.7 3.3 copy.18
  237.0 3.5 copy.19
  244.3 7.0 %collective-permute-done.18 = f32[1,128,16,256]{3,2,1,0:T(8,128)} collective-permute-done((f32[1,128,16,256]{3,2,1,0:T(8,128)}, f32[1,128,16,256]{3,2,1,0:T(8,128)}, u32[]{:S(2)}, u32[]{:S(2)}) %collective-permute-start.18) | collective-permute-done | bytes 2097184 | tf_op jit(solution)/shard_map/ppermute | solution.py:185
  255.4 56.1 %while.15 = (s32[]{:T(128)}, f32[128,16,256]{0,1,2:T(8,128)}, s32[4]{0:T(128)S(1)}, s32[4]{0:T(128)S(1)}, s32[256]{0:T(256)S(1)}, /*index=5*/f32[4,128,16,256]{1...) while((s32[]{:T(128)}, f32[128,16,256]{0,1,2:T(8,128)}, ...), condition=%wide.region_5.7_spmd.clone.clone, body=%wide.region_1.6_spmd.sunk.clone.clone.sunk | while | flops 2568969 | bytes 14700981 | solution.py:205
  259.9 3.0 dynamic-slice_bitcast_fusion.2
  272.8 3.0 dynamic-slice_bitcast_fusion.2
  278.4 4.2 %bitcast_add_fusion.2 = f32[128,16,256]{0,1,2:T(8,128)} fusion(f32[128,16,256]{0,1,2:T(8,128)} %get-tuple-element.350, f32[256,128,16]{1,2,0:T(8,128)S(1)} %gather_fusion, pred[256]{0:T(512)(128)(4,1)S(1)} %compare_reduce_fusion.2, pred[256]{0:T(512)(128)(4,1)S(1)} %compare_and_fusion.2, pred[]{:T(512)S(6)} %compare.119), kind=kLoop, calls=%fused_computation.2.clone.1 | loop fusion | flops 2097152 | bytes 6291969 | tf_op jit(solution)/shard_map/while/body/eval_jaxpr/add | solution.py:202
  287.2 3.0 dynamic-slice_bitcast_fusion.2
  292.8 4.2 %bitcast_add_fusion.2 = f32[128,16,256]{0,1,2:T(8,128)} fusion(f32[128,16,256]{0,1,2:T(8,128)} %get-tuple-element.350, f32[256,128,16]{1,2,0:T(8,128)S(1)} %gather_fusion, pred[256]{0:T(512)(128)(4,1)S(1)} %compare_reduce_fusion.2, pred[256]{0:T(512)(128)(4,1)S(1)} %compare_and_fusion.2, pred[]{:T(512)S(6)} %compare.119), kind=kLoop, calls=%fused_computation.2.clone.1 | loop fusion | flops 2097152 | bytes 6291969 | tf_op jit(solution)/shard_map/while/body/eval_jaxpr/add | solution.py:202
  307.2 4.2 %bitcast_add_fusion.2 = f32[128,16,256]{0,1,2:T(8,128)} fusion(f32[128,16,256]{0,1,2:T(8,128)} %get-tuple-element.350, f32[256,128,16]{1,2,0:T(8,128)S(1)} %gather_fusion, pred[256]{0:T(512)(128)(4,1)S(1)} %compare_reduce_fusion.2, pred[256]{0:T(512)(128)(4,1)S(1)} %compare_and_fusion.2, pred[]{:T(512)S(6)} %compare.119), kind=kLoop, calls=%fused_computation.2.clone.1 | loop fusion | flops 2097152 | bytes 6291969 | tf_op jit(solution)/shard_map/while/body/eval_jaxpr/add | solution.py:202
  327.9 4.6 %add_select_fusion.5 = f32[128,16,256]{2,1,0:T(8,128)S(1)} fusion(f32[128,16,256]{2,1,0:T(8,128)S(1)} %add_select_fusion.6, s32[]{:T(128)S(6)} %select_n.1335, s32[]{:T(128)S(6)} %select_n.1329, s32[]{:T(128)S(6)} %select_n.1331, s32[]{:T(128)S(6)} %select_n.1333, pred[256]{0:T(512)(128)(4,1)S(1)} %copy-done.29, pred[256]{0:T(512)(128)(4,1)S(1)} %copy-done.30, ...), kind=kLoop, calls=%fused_computation.268 | loop fusion | flops 5242880 | bytes 4195088 | tf_op jit(solution)/shard_map/jit(_where)/select_n | solution.py:98
  332.5 4.6 %add_select_fusion.4 = f32[128,16,256]{2,1,0:T(8,128)S(1)} fusion(f32[128,16,256]{2,1,0:T(8,128)S(1)} %add_select_fusion.5, s32[]{:T(128)S(6)} %select_n.1327, s32[]{:T(128)S(6)} %select_n.1321, s32[]{:T(128)S(6)} %select_n.1323, s32[]{:T(128)S(6)} %select_n.1325, pred[256]{0:T(512)(128)(4,1)S(1)} %copy-done.25, pred[256]{0:T(512)(128)(4,1)S(1)} %copy-done.26, ...), kind=kLoop, calls=%fused_computation.267 | loop fusion | flops 5242880 | bytes 4195088 | tf_op jit(solution)/shard_map/jit(_where)/select_n | solution.py:98
  337.1 4.8 %add_select_fusion.3 = f32[128,16,256]{2,1,0:T(8,128)S(1)} fusion(f32[128,16,256]{2,1,0:T(8,128)S(1)} %add_select_fusion.4, s32[]{:T(128)S(6)} %select_n.1319, s32[]{:T(128)S(6)} %select_n.1313, s32[]{:T(128)S(6)} %select_n.1315, s32[]{:T(128)S(6)} %select_n.1317, pred[256]{0:T(512)(128)(4,1)S(1)} %copy-done.23, pred[256]{0:T(512)(128)(4,1)S(1)} %copy-done.24, ...), kind=kLoop, calls=%fused_computation.266 | loop fusion | flops 5242880 | bytes 4195088 | tf_op jit(solution)/shard_map/jit(_where)/select_n | solution.py:98
  341.9 4.6 %add_select_fusion.2 = f32[128,16,256]{2,1,0:T(8,128)S(1)} fusion(f32[128,16,256]{2,1,0:T(8,128)S(1)} %add_select_fusion.3, s32[]{:T(128)S(6)} %select_n.1311, s32[]{:T(128)S(6)} %select_n.1305, s32[]{:T(128)S(6)} %select_n.1307, s32[]{:T(128)S(6)} %select_n.1309, pred[256]{0:T(512)(128)(4,1)S(1)} %copy-done.21, pred[256]{0:T(512)(128)(4,1)S(1)} %copy-done.22, ...), kind=kLoop, calls=%fused_computation.265 | loop fusion | flops 5242880 | bytes 4195088 | tf_op jit(solution)/shard_map/jit(_where)/select_n | solution.py:98
  346.6 4.8 %add_select_fusion.1 = f32[128,16,256]{2,1,0:T(8,128)S(1)} fusion(f32[128,16,256]{2,1,0:T(8,128)S(1)} %add_select_fusion.2, s32[]{:T(128)S(6)} %select_n.1303, s32[]{:T(128)S(6)} %select_n.1297, s32[]{:T(128)S(6)} %select_n.1299, s32[]{:T(128)S(6)} %select_n.1301, pred[256]{0:T(512)(128)(4,1)S(1)} %copy-done.17, pred[256]{0:T(512)(128)(4,1)S(1)} %copy-done.18, ...), kind=kLoop, calls=%fused_computation.264 | loop fusion | flops 5242880 | bytes 4195088 | tf_op jit(solution)/shard_map/jit(_where)/select_n | solution.py:98
  351.4 5.8 %fusion.24 = f32[1,128,16,256]{3,2,1,0:T(8,128)} fusion(f32[128,16,256]{2,1,0:T(8,128)S(1)} %add_select_fusion.1, s32[]{:T(128)S(6)} %select_n.1295, s32[]{:T(128)S(6)} %select_n.1289, s32[]{:T(128)S(6)} %select_n.1291, s32[]{:T(128)S(6)} %select_n.1293, pred[256]{0:T(512)(128)(4,1)S(1)} %copy-done.12, pred[256]{0:T(512)(128)(4,1)S(1)} %copy-done.13, ...), kind=kLoop, calls=%fused_computation.289 | loop fusion | flops 5242880 | bytes 4195088 | tf_op jit(solution)/shard_map/broadcast_in_dim | solution.py:206
  (209 shorter events, 117.9 us)
Async XLA Ops:
  0.7 22.6 %collective-permute-start = (f32[1,16,256]{2,1,0:T(8,128)S(1)}, f32[1,16,256]{2,1,0:T(8,128)S(1)}, u32[]{:S(2)}, u32[]{:S(2)}) collective-permute-start(f32[1,16,256]{2,1,0:T(8,128)S(1)} %get-tuple-element.260), channel_id=1, source_target_pairs={{4,0},{0,4},{5,1},{1,5},{6,2},{2,6},{7,3},{3,7},{12,8},{8,12},{13,... | collective-permute-start | bytes 49160 | tf_op jit(solution)/shard_map/ppermute | solution.py:20
  3.7 19.7 %collective-permute-start.1 = (f32[1,16,256]{2,1,0:T(8,128)S(1)}, f32[1,16,256]{2,1,0:T(8,128)S(1)}, u32[]{:S(2)}, u32[]{:S(2)}) collective-permute-start(f32[1,16,256]{2,1,0:T(8,128)S(1)} %get-tuple-element.259), channel_id=1, source_target_pairs={{0,4},{4,0},{1,5},{5,1},{2,6},{6,2},{3,7},{7,3},{8,12},{12,8},{9,1... | collective-permute-start | bytes 49160 | tf_op jit(solution)/shard_map/ppermute | solution.py:17
  3.7 5.1 %copy-start = (f32[1,128,16,256]{3,2,1,0:T(8,128)S(1)}, f32[1,128,16,256]{3,2,1,0:T(8,128)}, u32[]{:S(2)}) copy-start(f32[1,128,16,256]{3,2,1,0:T(8,128)} %param.10) | copy-start | bytes 6291460
  8.8 13.3 %copy-start.35 = (f32[2,4]{1,0:T(2,128)S(1)}, f32[2,4]{1,0:T(2,128)}, u32[]{:S(2)}) copy-start(f32[2,4]{1,0:T(2,128)} %param.13) | copy-start | bytes 100
  14.1 9.5 %copy-start.9 = (s32[256]{0:T(256)}, s32[256]{0:T(256)S(1)}, u32[]{:S(2)}) copy-start(s32[256]{0:T(256)S(1)} %get-tuple-element.226) | copy-start | bytes 3076
  24.0 12.4 %collective-permute-start.2 = (f32[130,1,256]{2,1,0:T(1,128)S(1)}, f32[130,1,256]{2,1,0:T(1,128)S(1)}, u32[]{:S(2)}, u32[]{:S(2)}) collective-permute-start(f32[130,1,256]{2,1,0:T(1,128)S(1)} %get-tuple-element.235), channel_id=1, source_target_pairs={{1,0},{2,1},{3,2},{0,3},{5,4},{6,5},{7,6},{4,7},{9,8},{10,9},{11,1... | collective-permute-start | bytes 399368 | tf_op jit(solution)/shard_map/ppermute | solution.py:20
  28.1 8.3 %collective-permute-start.3 = (f32[130,1,256]{2,1,0:T(1,128)S(1)}, f32[130,1,256]{2,1,0:T(1,128)}, u32[]{:S(2)}, u32[]{:S(2)}) collective-permute-start(f32[130,1,256]{2,1,0:T(1,128)S(1)} %get-tuple-element.236), channel_id=1, source_target_pairs={{0,1},{1,2},{2,3},{3,0},{4,5},{5,6},{6,7},{7,4},{8,9},{9,10},{10,1... | collective-permute-start | bytes 399368 | tf_op jit(solution)/shard_map/ppermute | solution.py:17
  51.9 3.8 %collective-permute-start.4 = (f32[1,16,256]{2,1,0:T(8,128)S(1)}, f32[1,16,256]{2,1,0:T(8,128)S(1)}, u32[]{:S(2)}, u32[]{:S(2)}) collective-permute-start(f32[1,16,256]{2,1,0:T(8,128)S(1)} %get-tuple-element.254), channel_id=1, source_target_pairs={{4,0},{0,4},{5,1},{1,5},{6,2},{2,6},{7,3},{3,7},{12,8},{8,12},{13,... | collective-permute-start | bytes 49160 | tf_op jit(solution)/shard_map/ppermute | solution.py:20
  53.5 3.7 %collective-permute-start.5 = (f32[1,16,256]{2,1,0:T(8,128)S(1)}, f32[1,16,256]{2,1,0:T(8,128)S(1)}, u32[]{:S(2)}, u32[]{:S(2)}) collective-permute-start(f32[1,16,256]{2,1,0:T(8,128)S(1)} %get-tuple-element.253), channel_id=1, source_target_pairs={{0,4},{4,0},{1,5},{5,1},{2,6},{6,2},{3,7},{7,3},{8,12},{12,8},{9,1... | collective-permute-start | bytes 49160 | tf_op jit(solution)/shard_map/ppermute | solution.py:17
  57.4 6.4 %collective-permute-start.6 = (f32[130,1,256]{2,1,0:T(1,128)S(1)}, f32[130,1,256]{2,1,0:T(1,128)S(1)}, u32[]{:S(2)}, u32[]{:S(2)}) collective-permute-start(f32[130,1,256]{2,1,0:T(1,128)S(1)} %get-tuple-element.233), channel_id=1, source_target_pairs={{1,0},{2,1},{3,2},{0,3},{5,4},{6,5},{7,6},{4,7},{9,8},{10,9},{11,1... | collective-permute-start | bytes 399368 | tf_op jit(solution)/shard_map/ppermute | solution.py:20
  61.3 7.2 %copy-start.7 = (pred[256]{0:T(512)(128)(4,1)S(1)}, pred[256]{0:T(512)(128)(4,1)}, u32[]{:S(2)}) copy-start(pred[256]{0:T(512)(128)(4,1)} %get-tuple-element.293) | copy-start | bytes 772
  61.3 7.2 %copy-start.8 = (pred[256]{0:T(512)(128)(4,1)S(1)}, pred[256]{0:T(512)(128)(4,1)}, u32[]{:S(2)}) copy-start(pred[256]{0:T(512)(128)(4,1)} %get-tuple-element.294) | copy-start | bytes 772
  61.3 7.2 %collective-permute-start.7 = (f32[130,1,256]{2,1,0:T(1,128)S(1)}, f32[130,1,256]{2,1,0:T(1,128)S(1)}, u32[]{:S(2)}, u32[]{:S(2)}) collective-permute-start(f32[130,1,256]{2,1,0:T(1,128)S(1)} %get-tuple-element.234), channel_id=1, source_target_pairs={{0,1},{1,2},{2,3},{3,0},{4,5},{5,6},{6,7},{7,4},{8,9},{9,10},{10,1... | collective-permute-start | bytes 399368 | tf_op jit(solution)/shard_map/ppermute | solution.py:17
  83.2 3.8 %collective-permute-start.8 = (f32[1,16,256]{2,1,0:T(8,128)S(1)}, f32[1,16,256]{2,1,0:T(8,128)S(1)}, u32[]{:S(2)}, u32[]{:S(2)}) collective-permute-start(f32[1,16,256]{2,1,0:T(8,128)S(1)} %get-tuple-element.248), channel_id=1, source_target_pairs={{4,0},{0,4},{5,1},{1,5},{6,2},{2,6},{7,3},{3,7},{12,8},{8,12},{13,... | collective-permute-start | bytes 49160 | tf_op jit(solution)/shard_map/ppermute | solution.py:20
  83.8 3.7 %collective-permute-start.9 = (f32[1,16,256]{2,1,0:T(8,128)S(1)}, f32[1,16,256]{2,1,0:T(8,128)S(1)}, u32[]{:S(2)}, u32[]{:S(2)}) collective-permute-start(f32[1,16,256]{2,1,0:T(8,128)S(1)} %get-tuple-element.247), channel_id=1, source_target_pairs={{0,4},{4,0},{1,5},{5,1},{2,6},{6,2},{3,7},{7,3},{8,12},{12,8},{9,1... | collective-permute-start | bytes 49160 | tf_op jit(solution)/shard_map/ppermute | solution.py:17
  87.8 5.0 %collective-permute-start.10 = (f32[130,1,256]{2,1,0:T(1,128)S(1)}, f32[130,1,256]{2,1,0:T(1,128)S(1)}, u32[]{:S(2)}, u32[]{:S(2)}) collective-permute-start(f32[130,1,256]{2,1,0:T(1,128)S(1)} %get-tuple-element.231), channel_id=1, source_target_pairs={{1,0},{2,1},{3,2},{0,3},{5,4},{6,5},{7,6},{4,7},{9,8},{10,9},{11,1... | collective-permute-start | bytes 399368 | tf_op jit(solution)/shard_map/ppermute | solution.py:20
  87.8 6.8 %collective-permute-start.11 = (f32[130,1,256]{2,1,0:T(1,128)S(1)}, f32[130,1,256]{2,1,0:T(1,128)S(1)}, u32[]{:S(2)}, u32[]{:S(2)}) collective-permute-start(f32[130,1,256]{2,1,0:T(1,128)S(1)} %get-tuple-element.232), channel_id=1, source_target_pairs={{0,1},{1,2},{2,3},{3,0},{4,5},{5,6},{6,7},{7,4},{8,9},{9,10},{10,1... | collective-permute-start | bytes 399368 | tf_op jit(solution)/shard_map/ppermute | solution.py:17
  109.4 3.8 %collective-permute-start.12 = (f32[1,16,256]{2,1,0:T(8,128)S(1)}, f32[1,16,256]{2,1,0:T(8,128)S(1)}, u32[]{:S(2)}, u32[]{:S(2)}) collective-permute-start(f32[1,16,256]{2,1,0:T(8,128)S(1)} %get-tuple-element.242), channel_id=1, source_target_pairs={{4,0},{0,4},{5,1},{1,5},{6,2},{2,6},{7,3},{3,7},{12,8},{8,12},{13,... | collective-permute-start | bytes 49160 | tf_op jit(solution)/shard_map/ppermute | solution.py:20
  110.9 3.7 %collective-permute-start.13 = (f32[1,16,256]{2,1,0:T(8,128)S(1)}, f32[1,16,256]{2,1,0:T(8,128)S(1)}, u32[]{:S(2)}, u32[]{:S(2)}) collective-permute-start(f32[1,16,256]{2,1,0:T(8,128)S(1)} %get-tuple-element.241), channel_id=1, source_target_pairs={{0,4},{4,0},{1,5},{5,1},{2,6},{6,2},{3,7},{7,3},{8,12},{12,8},{9,1... | collective-permute-start | bytes 49160 | tf_op jit(solution)/shard_map/ppermute | solution.py:17
  114.9 5.0 %collective-permute-start.14 = (f32[130,1,256]{2,1,0:T(1,128)S(1)}, f32[130,1,256]{2,1,0:T(1,128)S(1)}, u32[]{:S(2)}, u32[]{:S(2)}) collective-permute-start(f32[130,1,256]{2,1,0:T(1,128)S(1)} %get-tuple-element.229), channel_id=1, source_target_pairs={{1,0},{2,1},{3,2},{0,3},{5,4},{6,5},{7,6},{4,7},{9,8},{10,9},{11,1... | collective-permute-start | bytes 399368 | tf_op jit(solution)/shard_map/ppermute | solution.py:20
  114.9 6.8 %collective-permute-start.15 = (f32[130,1,256]{2,1,0:T(1,128)S(1)}, f32[130,1,256]{2,1,0:T(1,128)S(1)}, u32[]{:S(2)}, u32[]{:S(2)}) collective-permute-start(f32[130,1,256]{2,1,0:T(1,128)S(1)} %get-tuple-element.230), channel_id=1, source_target_pairs={{0,1},{1,2},{2,3},{3,0},{4,5},{5,6},{6,7},{7,4},{8,9},{9,10},{10,1... | collective-permute-start | bytes 399368 | tf_op jit(solution)/shard_map/ppermute | solution.py:17
  121.8 14.9 %copy-start.11 = (pred[256]{0:T(512)(128)(4,1)S(1)}, pred[256]{0:T(512)(128)(4,1)}, u32[]{:S(2)}) copy-start(pred[256]{0:T(512)(128)(4,1)} %get-tuple-element.272) | copy-start | bytes 772
  121.8 14.9 %copy-start.12 = (pred[256]{0:T(512)(128)(4,1)S(1)}, pred[256]{0:T(512)(128)(4,1)}, u32[]{:S(2)}) copy-start(pred[256]{0:T(512)(128)(4,1)} %get-tuple-element.291) | copy-start | bytes 772
  121.8 14.9 %copy-start.13 = (pred[256]{0:T(512)(128)(4,1)S(1)}, pred[256]{0:T(512)(128)(4,1)}, u32[]{:S(2)}) copy-start(pred[256]{0:T(512)(128)(4,1)} %get-tuple-element.292) | copy-start | bytes 772
  146.0 4.9 %copy-start.19 = (pred[256]{0:T(512)(128)(4,1)S(1)}, pred[256]{0:T(512)(128)(4,1)}, u32[]{:S(2)}) copy-start(pred[256]{0:T(512)(128)(4,1)} %get-tuple-element.269) | copy-start | bytes 772
  146.0 4.9 %copy-start.23 = (pred[256]{0:T(512)(128)(4,1)S(1)}, pred[256]{0:T(512)(128)(4,1)}, u32[]{:S(2)}) copy-start(pred[256]{0:T(512)(128)(4,1)} %get-tuple-element.285) | copy-start | bytes 772
  160.3 5.0 %copy-start.27 = (pred[256]{0:T(512)(128)(4,1)S(1)}, pred[256]{0:T(512)(128)(4,1)}, u32[]{:S(2)}) copy-start(pred[256]{0:T(512)(128)(4,1)} %get-tuple-element.267) | copy-start | bytes 772
  177.0 48.6 %copy-start.10 = (s32[256]{0:T(256)S(1)}, s32[256]{0:T(256)}, u32[]{:S(2)}) copy-start(s32[256]{0:T(256)} %copy-done.9) | copy-start | bytes 3076
  177.0 48.6 %copy-start.6 = (s32[49]{0:T(128)S(1)}, s32[49]{0:T(128)}, u32[]{:S(2)}) copy-start(s32[49]{0:T(128)} %constant.625.clone) | copy-start | bytes 592
  179.3 46.3 %collective-permute-start.16 = (f32[1,128,16,256]{3,2,1,0:T(8,128)S(1)}, f32[1,128,16,256]{3,2,1,0:T(8,128)}, u32[]{:S(2)}, u32[]{:S(2)}) collective-permute-start(f32[1,128,16,256]{3,2,1,0:T(8,128)S(1)} %fusion.23), channel_id=1, source_target_pairs={{0,8},{8,16},{16,24},{24,0},{1,9},{9,17},{17,25},{25,1},{2,10},{10... | collective-permute-start | bytes 6291464 | tf_op jit(solution)/shard_map/ppermute | solution.py:185
  179.4 57.6 %collective-permute-start.17 = (f32[1,128,16,256]{3,2,1,0:T(8,128)S(1)}, f32[1,128,16,256]{3,2,1,0:T(8,128)}, u32[]{:S(2)}, u32[]{:S(2)}) collective-permute-start(f32[1,128,16,256]{3,2,1,0:T(8,128)S(1)} %fusion.23), channel_id=1, source_target_pairs={{0,24},{8,0},{16,8},{24,16},{1,25},{9,1},{17,9},{25,17},{2,26},{10... | collective-permute-start | bytes 6291464 | tf_op jit(solution)/shard_map/ppermute | solution.py:188
  225.6 25.8 %collective-permute-start.18 = (f32[1,128,16,256]{3,2,1,0:T(8,128)}, f32[1,128,16,256]{3,2,1,0:T(8,128)}, u32[]{:S(2)}, u32[]{:S(2)}) collective-permute-start(f32[1,128,16,256]{3,2,1,0:T(8,128)} %collective-permute-done.16), channel_id=1, source_target_pairs={{0,8},{8,16},{16,24},{24,0},{1,9},{9,17},{17,25},{25,1},{2,10},{10... | collective-permute-start | bytes 6291464 | tf_op jit(solution)/shard_map/ppermute | solution.py:185
  (25 other events, 86.3 us)
